TPU v7x, 32 devices: a whole 2x2x4 slice. The times are simulated.
32 devices in a mesh: row: 4 (over z), col: 8 (over y, x, core).
Axes of the slice: x: 2, y: 2, z: 4, core: 2. Of those that a mesh axis runs over, the one named last changes fastest.
Arguments:
- state_start: bfloat16 [512, 2048], P('row', 'col'), may hold values from -360 to 360
- actions: int32 [512, 2], P('row'), may hold values from 0 to 17
- targets: bfloat16 [2, 512, 2048], P(None, 'row'), may hold values from -504 to 504
- w_in: bfloat16 [2048, 4096], P('row', 'col'), may hold values from -0.125 to 0.125
- w_out: bfloat16 [4096, 2048], P('col', 'row'), may hold values from -0.09375 to 0.09375
- action_embed: bfloat16 [18, 4096], P(None, 'col'), may hold values from -6 to 6
Outputs:
- grad_w_in: float32 [2048, 4096], P('row', 'col')
- grad_w_out: float32 [4096, 2048], P('col', 'row')
All inputs are finite; a program needn't handle non-finite values.
Results may differ from a plain program's by a relative error of at most 0.035.
Values may be sent and summed in bfloat16 or wider, within the bound.
A program may use at most 64 MiB of HBM per device.

v0:
```python
import jax
import jax.numpy as jnp
from jax import lax
from jax.sharding import PartitionSpec as P

EPS = 1e-06
LOSS_SCALE = 128.0


def silu_grad(pre_act):
    gate_val = jax.nn.sigmoid(pre_act)
    return gate_val * (1.0 + pre_act * (1.0 - gate_val))


def cosine_from(state_f, target_f, self_dot, cross_dot, target_dot):
    inv_state = lax.rsqrt(self_dot + EPS)
    inv_target = lax.rsqrt(target_dot + EPS)
    cosine = cross_dot * inv_state * inv_target
    return -LOSS_SCALE * (
        target_f * inv_state * inv_target - cosine * state_f * inv_state * inv_state
    )


def shared_cosine(state, target):
    state_f = state.astype(jnp.float32)
    target_f = target.astype(jnp.float32)
    self_dot, cross_dot, target_dot = lax.psum(
        (
            jnp.sum(state_f * state_f, axis=-1),
            jnp.sum(state_f * target_f, axis=-1),
            jnp.sum(target_f * target_f, axis=-1),
        ),
        "col",
    )
    return cosine_from(
        state_f, target_f, self_dot[:, None], cross_dot[:, None], target_dot[:, None]
    )


def on_device(state_start, actions, targets, w_in, w_out, action_embed):
    unroll_steps = targets.shape[0]
    col_width = state_start.shape[1]
    w_in_panel = lax.all_gather(w_in, "row", axis=0, tiled=True)
    w_out_panel = lax.all_gather(w_out, "row", axis=1, tiled=True)
    col_start = lax.axis_index("col") * col_width
    action_ids = jnp.arange(action_embed.shape[0], dtype=jnp.int32)
    contract_last = (((1,), (1,)), ((), ()))
    current = state_start
    full_states = []
    pre_list = []
    hidden_list = []
    cos_terms = []
    for unroll in range(unroll_steps):
        full_rows = lax.all_gather(current, "col", axis=1, tiled=True)
        onehot = (actions[:, unroll][:, None] == action_ids[None, :]).astype(jnp.bfloat16)
        pre_act = jnp.dot(full_rows, w_in_panel, preferred_element_type=jnp.float32) + jnp.dot(
            onehot, action_embed, preferred_element_type=jnp.float32
        )
        hidden = jax.nn.silu(pre_act).astype(jnp.bfloat16)
        partial_value = jnp.dot(hidden, w_out_panel, preferred_element_type=jnp.float32)
        target = targets[unroll]
        branch = lax.psum_scatter(
            partial_value.astype(jnp.bfloat16), "col", scatter_dimension=1, tiled=True
        ).astype(jnp.float32)
        current = (current.astype(jnp.float32) + branch).astype(jnp.bfloat16)
        target_slice = lax.dynamic_slice_in_dim(target, col_start, col_width, 1)
        cos_terms.append(shared_cosine(current, target_slice))
        full_states.append(full_rows)
        pre_list.append(pre_act)
        hidden_list.append(hidden)
    state_grad = cos_terms[unroll_steps - 1].astype(jnp.bfloat16)
    grad_list = [None] * unroll_steps
    hid_grads = [None] * unroll_steps
    for unroll in reversed(range(unroll_steps)):
        grad_rows = lax.all_gather(state_grad, "col", axis=1, tiled=True)
        back = lax.dot_general(
            grad_rows, w_out_panel, contract_last, preferred_element_type=jnp.float32
        )
        hid_grad = (back * silu_grad(pre_list[unroll])).astype(jnp.bfloat16)
        grad_list[unroll] = grad_rows
        hid_grads[unroll] = hid_grad
        if unroll > 0:
            input_part = lax.dot_general(
                hid_grad, w_in_panel, contract_last, preferred_element_type=jnp.float32
            )
            summed = lax.psum_scatter(
                input_part.astype(jnp.bfloat16), "col", scatter_dimension=1, tiled=True
            ).astype(jnp.float32)
            state_grad = (state_grad.astype(jnp.float32) + summed + cos_terms[unroll - 1]).astype(
                jnp.bfloat16
            )
    grad_stack = jnp.stack(grad_list)
    hidden_stack = jnp.stack(hidden_list)
    state_stack = jnp.stack(full_states)
    hid_stack = jnp.stack(hid_grads)
    grad_feature_blocks = lax.all_to_all(grad_stack, "row", split_axis=2, concat_axis=1, tiled=True)
    hidden_all = lax.all_gather(hidden_stack, "row", axis=1, tiled=True)
    grad_w_out = jnp.einsum(
        "kbf,kbd->fd", hidden_all, grad_feature_blocks, preferred_element_type=jnp.float32
    )
    state_feature_blocks = lax.all_to_all(
        state_stack, "row", split_axis=2, concat_axis=1, tiled=True
    )
    hid_all = lax.all_gather(hid_stack, "row", axis=1, tiled=True)
    grad_w_in = jnp.einsum(
        "kbd,kbf->df", state_feature_blocks, hid_all, preferred_element_type=jnp.float32
    )
    return (grad_w_in, grad_w_out)


def solution(mesh):
    in_specs = (
        P("row", "col"),
        P("row", None),
        P(None, "row", None),
        P("row", "col"),
        P("col", "row"),
        P(None, "col"),
    )
    out_specs = (P("row", "col"), P("col", "row"))
    return jax.shard_map(
        on_device, mesh=mesh, in_specs=in_specs, out_specs=out_specs, check_vma=False
    )
```

profile of v0, /device:TPU:0, one launch (start us, length us, event | category | flops | bytes accessed | tf_op | source)
XLA Modules:
  0.0 336.0 jit_solution(11510671725148091114)
XLA Ops:
  8.7 12.7 %all_gather.24 = bf16[128,2048]{1,0:T(8,128)(2,1)S(1)} all-gather(bf16[128,256]{1,0:T(8,128)(2,1)} %param.6), channel_id=1, replica_groups=mesh['row'=4,'col'=8] {'col'}, dimensions={1}, use_global_device_ids=true | all-gather | bytes 589824 | tf_op jit(solution)/shard_map/all_gather | solution.py:54
  22.4 35.6 %all-gather.5.cloned.1.call-done = bf16[2048,512]{1,0:T(8,128)(2,1)} async-done(((bf16[512,512]{1,0:T(8,128)(2,1)}), bf16[2048,512]{1,0:T(8,128)(2,1)}) %all-gather.5.cloned.1.call-update) | async-done | bytes 2097168 | tf_op jit(solution)/shard_map/all_gather | solution.py:43
  58.0 2.0 convolution_add_fusion.1
  60.0 44.0 %all-gather.7.cloned.1.call-done = bf16[512,2048]{1,0:T(8,128)(2,1)} async-done(((bf16[512,512]{1,0:T(8,128)(2,1)}), bf16[512,2048]{1,0:T(8,128)(2,1)}) %all-gather.7.cloned.1.call-update) | async-done | bytes 2097168 | tf_op jit(solution)/shard_map/all_gather | solution.py:44
  104.0 2.9 convolution_convert_fusion.2
  107.9 2.1 fusion.29
  110.0 30.6 %reduce-scatter.4.cloned.1.call-done = bf16[128,256]{1,0:T(8,128)(2,1)} async-done(((bf16[128,2048]{1,0:T(8,128)(2,1)}), bf16[128,256]{1,0:T(8,128)(2,1)}) %reduce-scatter.4.cloned.1.call-update) | async-done | bytes 65552 | tf_op jit(solution)/shard_map/reduce_scatter | solution.py:62
  141.8 10.9 %all_gather.27 = bf16[128,2048]{1,0:T(8,128)(2,1)S(1)} all-gather(bf16[128,256]{1,0:T(8,128)(2,1)S(1)} %get-tuple-element.14), channel_id=1, replica_groups=mesh['row'=4,'col'=8] {'col'}, dimensions={1}, use_global_device_ids=true | all-gather | bytes 589824 | tf_op jit(solution)/shard_map/all_gather | solution.py:54
  152.7 2.1 convolution_add_fusion
  154.8 2.2 convolution_convert_fusion.1
  157.1 34.2 %reduce-scatter.6.cloned.1.call-done = bf16[128,256]{1,0:T(8,128)(2,1)} async-done(((bf16[128,2048]{1,0:T(8,128)(2,1)}), bf16[128,256]{1,0:T(8,128)(2,1)}) %reduce-scatter.6.cloned.1.call-update) | async-done | bytes 65552 | tf_op jit(solution)/shard_map/reduce_scatter | solution.py:62
  192.3 12.1 %all-reduce = (f32[128]{0:T(128)S(1)}, f32[128]{0:T(128)S(1)}, f32[128]{0:T(128)S(1)}, f32[128]{0:T(128)S(1)}, f32[128]{0:T(128)S(1)}, /*index=5*/f32[128]{0:T(128)S(1)}) all-reduce(f32[128]{0:T(128)S(1)} %get-tuple-element.5, f32[128]{0:T(128)S(1)} %get-tuple-element.6, ...), channel_id=1, replica_groups=mesh['row'=4,'col'=8] {'col'}, use_global_device_ids=true, to_apply=%region_7.8 | all-reduce | flops 768 | bytes 6144 | tf_op jit(solution)/shard_map/psum | solution.py:27
  206.1 10.9 %all_gather.28 = bf16[128,2048]{1,0:T(8,128)(2,1)S(1)} all-gather(bf16[128,256]{1,0:T(8,128)(2,1)S(1)} %fusion.8), channel_id=1, replica_groups=mesh['row'=4,'col'=8] {'col'}, dimensions={1}, use_global_device_ids=true | all-gather | bytes 589824 | tf_op jit(solution)/shard_map/all_gather | solution.py:75
  217.8 2.4 fusion
  222.6 2.0 copy.11
  224.6 4.9 %all-to-all-start = ((bf16[2,128,2048]{1,0,2:T(2,128)(2,1)}), bf16[2,128,2048]{1,0,2:T(2,128)(2,1)S(1)}, u32[]{:S(2)}, u32[]{:S(2)}) async-start(bf16[2,128,2048]{1,0,2:T(2,128)(2,1)} %copy.11), calls=%async_computation.1 | async-start | bytes 2097152 | tf_op jit(solution)/shard_map/all_to_all | solution.py:101
  231.4 25.5 %reduce-scatter.8.cloned.1.call-done = bf16[128,256]{1,0:T(8,128)(2,1)} async-done(((bf16[128,2048]{1,0:T(8,128)(2,1)}), bf16[128,256]{1,0:T(8,128)(2,1)}) %reduce-scatter.8.cloned.1.call-update) | async-done | bytes 65552 | tf_op jit(solution)/shard_map/reduce_scatter | solution.py:86
  258.0 10.9 %all_gather.29 = bf16[128,2048]{1,0:T(8,128)(2,1)S(1)} all-gather(bf16[128,256]{1,0:T(8,128)(2,1)S(1)} %fusion.16), channel_id=1, replica_groups=mesh['row'=4,'col'=8] {'col'}, dimensions={1}, use_global_device_ids=true | all-gather | bytes 589824 | tf_op jit(solution)/shard_map/all_gather | solution.py:75
  271.0 4.6 %all-to-all-start.1 = ((bf16[2,128,2048]{1,0,2:T(2,128)(2,1)}), bf16[2,128,2048]{1,0,2:T(2,128)(2,1)S(1)}, u32[]{:S(2)}, u32[]{:S(2)}) async-start(bf16[2,128,2048]{1,0,2:T(2,128)(2,1)} %copy.13), calls=%async_computation.4 | async-start | bytes 2097152 | tf_op jit(solution)/shard_map/all_to_all | solution.py:96
  275.6 2.5 fusion.2
  280.1 33.4 %all-to-all-done.1 = bf16[2,128,2048]{1,0,2:T(2,128)(2,1)S(1)} async-done(((bf16[2,128,2048]{1,0,2:T(2,128)(2,1)}), bf16[2,128,2048]{1,0,2:T(2,128)(2,1)S(1)}, u32[]{:S(2)}, u32[]{:S(2)}) %all-to-all-start.1) | async-done | bytes 1048608 | tf_op jit(solution)/shard_map/all_to_all | solution.py:96
  314.3 2.9 convolution_bitcast_fusion
  317.2 9.0 %all-gather.9.cloned.1.call-done = bf16[2,512,512]{2,1,0:T(8,128)(2,1)} async-done(((bf16[2,128,512]{2,1,0:T(8,128)(2,1)}), bf16[2,512,512]{2,1,0:T(8,128)(2,1)}) %all-gather.9.cloned.1.call-update) | async-done | bytes 1048592 | tf_op jit(solution)/shard_map/all_gather | solution.py:104
  326.2 2.9 convolution_bitcast_fusion.1
  (56 shorter events, 18.3 us)
Async XLA Ops:
  7.2 15.0 %copy-start = (bf16[18,512]{1,0:T(8,128)(2,1)S(1)}, bf16[18,512]{1,0:T(8,128)(2,1)}, u32[]{:S(2)}) copy-start(bf16[18,512]{1,0:T(8,128)(2,1)} %param.11) | copy-start | bytes 55300
  7.2 50.8 %all-gather.5.cloned.1.call-start = ((), (), s32[]{:S(2)}) async-start(), calls=%async_computation.5 | async-start | bytes 2621440 | tf_op jit(solution)/shard_map/all_gather | solution.py:43
  7.9 96.1 %all-gather.7.cloned.1.call-start = ((), (), s32[]{:S(2)}) async-start(), calls=%async_computation.6 | async-start | bytes 2621440 | tf_op jit(solution)/shard_map/all_gather | solution.py:44
  8.7 132.0 %reduce-scatter.4.cloned.1.call-start = ((), (), s32[]{:S(2)}) async-start(), calls=%async_computation.7 | async-start | bytes 589824 | tf_op jit(solution)/shard_map/reduce_scatter | solution.py:62
  106.9 45.8 %copy-start.1 = (bf16[2048,512]{1,0:T(8,128)(2,1)S(1)}, bf16[2048,512]{1,0:T(8,128)(2,1)}, u32[]{:S(2)}) copy-start(bf16[2048,512]{1,0:T(8,128)(2,1)} %all-gather.5.cloned.1.call-done) | copy-start | bytes 6291460
  106.9 84.4 %reduce-scatter.6.cloned.1.call-start = ((), (), s32[]{:S(2)}) async-start(), calls=%async_computation.8 | async-start | bytes 589824 | tf_op jit(solution)/shard_map/reduce_scatter | solution.py:62
  110.0 31.7 %copy-start.4 = (bf16[1,128,2048]{2,1,0:T(8,128)(2,1)}, bf16[1,128,2048]{2,1,0:T(8,128)(2,1)S(1)}, u32[]{:S(2)}) copy-start(bf16[1,128,2048]{2,1,0:T(8,128)(2,1)S(1)} %get-tuple-element.16) | copy-start | bytes 1572868
  140.6 14.2 %copy-start.9 = (bf16[512,2048]{1,0:T(8,128)(2,1)S(1)}, bf16[512,2048]{1,0:T(8,128)(2,1)}, u32[]{:S(2)}) copy-start(bf16[512,2048]{1,0:T(8,128)(2,1)} %all-gather.7.cloned.1.call-done) | copy-start | bytes 6291460
  157.0 99.9 %reduce-scatter.8.cloned.1.call-start = ((), (), s32[]{:S(2)}) async-start(), calls=%async_computation.9 | async-start | bytes 589824 | tf_op jit(solution)/shard_map/reduce_scatter | solution.py:86
  205.5 0.6 copy-start.5
  217.0 0.8 copy-start.2
  220.2 0.6 copy-start.7
  224.6 32.3 %copy-start.6 = (bf16[128,256]{1,0:T(8,128)(2,1)S(1)}, bf16[128,256]{1,0:T(8,128)(2,1)}, u32[]{:S(2)}) copy-start(bf16[128,256]{1,0:T(8,128)(2,1)} %copy-done.5) | copy-start | bytes 196612
  224.6 44.2 %copy-start.3 = (bf16[128,2048]{1,0:T(8,128)(2,1)S(1)}, bf16[128,2048]{1,0:T(8,128)(2,1)}, u32[]{:S(2)}) copy-start(bf16[128,2048]{1,0:T(8,128)(2,1)} %copy-done.2) | copy-start | bytes 1572868
  224.6 46.3 %all-to-all-start = ((bf16[2,128,2048]{1,0,2:T(2,128)(2,1)}), bf16[2,128,2048]{1,0,2:T(2,128)(2,1)S(1)}, u32[]{:S(2)}, u32[]{:S(2)}) async-start(bf16[2,128,2048]{1,0,2:T(2,128)(2,1)} %copy.11), calls=%async_computation.1 | async-start | bytes 2097152 | tf_op jit(solution)/shard_map/all_to_all | solution.py:101
  229.5 84.8 %all-gather.11.cloned.1.call-start = ((), (), s32[]{:S(2)}) async-start(), calls=%async_computation.11 | async-start | bytes 1310720 | tf_op jit(solution)/shard_map/all_gather | solution.py:97
  271.0 42.5 %all-to-all-start.1 = ((bf16[2,128,2048]{1,0,2:T(2,128)(2,1)}), bf16[2,128,2048]{1,0,2:T(2,128)(2,1)S(1)}, u32[]{:S(2)}, u32[]{:S(2)}) async-start(bf16[2,128,2048]{1,0,2:T(2,128)(2,1)} %copy.13), calls=%async_computation.4 | async-start | bytes 2097152 | tf_op jit(solution)/shard_map/all_to_all | solution.py:96
  275.6 2.5 copy-start.8
  275.6 50.7 %all-gather.9.cloned.1.call-start = ((), (), s32[]{:S(2)}) async-start(), calls=%async_computation.10 | async-start | bytes 1310720 | tf_op jit(solution)/shard_map/all_gather | solution.py:104
Sparse Core Ops, SparseCore 0:
  9.6 48.3 all-gather.4
  59.5 44.4 all-gather.6
  107.7 32.8 reduce-scatter.3
  157.1 34.0 reduce-scatter.5
  222.6 34.2 reduce-scatter.7
  258.4 37.5 all-gather.10
  297.5 28.6 all-gather.8
where the time goes:
time: 337 us; the launch traced here: 336 us
  waiting for transfers between devices  214 us (64%)
  blocking collectives  57.5 us (17%)
  matrix products  22.8 us (7%)
  between operations  14.3 us (4%)
  local copies, waits for them, and re-layouts  11 us (3%)
  starting transfers between devices  9.7 us (3%)
  other arithmetic  6.97 us (2%)
    reduce_scatter x2, waiting for transfers between devices, on_device(): lax.psum_scatter(partial_value.astype(jnp.bfloat16), 'col', scatter_dimen...  64.8 us
    all_gather x1, waiting for transfers between devices, on_device(): w_out_panel = lax.all_gather(w_out, 'row', axis=1, tiled=True)  44 us
    all_gather x1, waiting for transfers between devices, on_device(): w_in_panel = lax.all_gather(w_in, 'row', axis=0, tiled=True)  35.6 us
    all_to_all x1, waiting for transfers between devices, on_device(): lax.all_to_all(grad_stack, 'row', split_axis=2, concat_axis=1, tiled=True)  33.4 us
    reduce_scatter x1, waiting for transfers between devices, on_device(): lax.psum_scatter(input_part.astype(jnp.bfloat16), 'col', scatter_dimensio...  25.5 us
    all_gather x2, blocking collectives, on_device(): full_rows = lax.all_gather(current, 'col', axis=1, tiled=True)  23.6 us
    all_gather x2, blocking collectives, on_device(): grad_rows = lax.all_gather(state_grad, 'col', axis=1, tiled=True)  21.8 us
    psum x1, blocking collectives, shared_cosine(): lax.psum((jnp.sum(state_f * state_f, axis=-1), jnp.sum(state_f * target_f...  12.1 us
  transfers between devices with their start and end apart: 9, of which 7 were waited for; matrix products, arithmetic and copies ran while one was open for 6% of the time, Pallas kernels for 0%

commit v1 on v0

--- a/solution.py
+++ b/solution.py
@@ -5,6 +5,24 @@
 
 EPS = 1e-06
 LOSS_SCALE = 128.0
+
+
+def ring_gather(array, axis, dim):
+    ways, here, turn = (lax.axis_size(axis), lax.axis_index(axis), array.shape[dim])
+    shape = [n * ways if d == dim else n for d, n in enumerate(array.shape)]
+    full = lax.dynamic_update_slice_in_dim(
+        jnp.zeros(shape, array.dtype), array, here * turn, axis=dim
+    )
+    going_up = going_down = array
+    for far in range(1, ways // 2 + 1):
+        going_up = lax.ppermute(going_up, axis, [(d, (d + 1) % ways) for d in range(ways)])
+        full = lax.dynamic_update_slice_in_dim(full, going_up, (here - far) % ways * turn, axis=dim)
+        if 2 * far < ways:
+            going_down = lax.ppermute(going_down, axis, [(d, (d - 1) % ways) for d in range(ways)])
+            full = lax.dynamic_update_slice_in_dim(
+                full, going_down, (here + far) % ways * turn, axis=dim
+            )
+    return full
 
 
 def silu_grad(pre_act):
@@ -41,7 +59,7 @@
     unroll_steps = targets.shape[0]
     col_width = state_start.shape[1]
     w_in_panel = lax.all_gather(w_in, "row", axis=0, tiled=True)
-    w_out_panel = lax.all_gather(w_out, "row", axis=1, tiled=True)
+    w_out_panel = ring_gather(w_out, "row", 1)
     col_start = lax.axis_index("col") * col_width
     action_ids = jnp.arange(action_embed.shape[0], dtype=jnp.int32)
     contract_last = (((1,), (1,)), ((), ()))

time: 337 us -> 315 us (0.935)
  waiting for transfers between devices: 214 us -> 181 us
  starting transfers between devices: 9.7 us -> 23.5 us
  blocking collectives: 57.5 us -> 53.3 us
    all_gather x1 -> x0, waiting for transfers between devices: 44 us -> none  [on_device(): w_out_panel = lax.all_gather(w_out, 'row', axis=1, tiled=True)]
    ppermute x0 -> x3, waiting for transfers between devices: none -> 37.8 us  [the longest x1 20.7 us: ring_gather(): lax.ppermute(going_down, axis, [(d, (d - 1) % ways) for d in range(ways)])]
    all_gather x1, waiting for transfers between devices: 35.6 us -> 10 us  [on_device(): w_in_panel = lax.all_gather(w_in, 'row', axis=0, tiled=True)]
    ppermute x0 -> x3, starting transfers between devices: none -> 13.8 us  [the longest x2 11.7 us: ring_gather(): lax.ppermute(going_up, axis, [(d, (d + 1) % ways) for d in range(ways)])]
    all_gather x2, blocking collectives: 23.6 us -> 19.5 us  [on_device(): full_rows = lax.all_gather(current, 'col', axis=1, tiled=True)]
  transfers between devices with their start and end apart: 9 -> 11, of which waited for: 7 -> 9; matrix products, arithmetic and copies ran while one was open for 6% -> 7% of each run, Pallas kernels for 0% -> 0%
where the time goes in v1:
time: 315 us; the launch traced here: 314 us
  waiting for transfers between devices  181 us (57%)
  blocking collectives  53.3 us (17%)
  starting transfers between devices  23.5 us (7%)
  matrix products  21.1 us (7%)
  between operations  14.3 us (5%)
  local copies, waits for them, and re-layouts  13.6 us (4%)
  other arithmetic  6.96 us (2%)
    reduce_scatter x2, waiting for transfers between devices, on_device(): lax.psum_scatter(partial_value.astype(jnp.bfloat16), 'col', scatter_dimen...  64.9 us
    all_to_all x1, waiting for transfers between devices, on_device(): lax.all_to_all(grad_stack, 'row', split_axis=2, concat_axis=1, tiled=True)  33.8 us
    reduce_scatter x1, waiting for transfers between devices, on_device(): lax.psum_scatter(input_part.astype(jnp.bfloat16), 'col', scatter_dimensio...  25.5 us
    all_gather x2, blocking collectives, on_device(): grad_rows = lax.all_gather(state_grad, 'col', axis=1, tiled=True)  21.7 us
    ppermute x1, waiting for transfers between devices, ring_gather(): lax.ppermute(going_down, axis, [(d, (d - 1) % ways) for d in range(ways)])  20.7 us
    all_gather x2, blocking collectives, on_device(): full_rows = lax.all_gather(current, 'col', axis=1, tiled=True)  19.5 us
    ppermute x2, waiting for transfers between devices, ring_gather(): lax.ppermute(going_up, axis, [(d, (d + 1) % ways) for d in range(ways)])  17.1 us
    psum x1, blocking collectives, shared_cosine(): lax.psum((jnp.sum(state_f * state_f, axis=-1), jnp.sum(state_f * target_f...  12.2 us
  transfers between devices with their start and end apart: 11, of which 9 were waited for; matrix products, arithmetic and copies ran while one was open for 7% of the time, Pallas kernels for 0%

profile of v1, /device:TPU:0, one launch (start us, length us, event | category | flops | bytes accessed | tf_op | source)
XLA Modules:
  0.0 314.3 jit_solution(18094225277210010467)
XLA Ops:
  8.0 3.1 collective-permute-start
  14.3 13.5 %collective-permute-done = bf16[512,512]{1,0:T(8,128)(2,1)} collective-permute-done((bf16[512,512]{1,0:T(8,128)(2,1)}, bf16[512,512]{1,0:T(8,128)(2,1)}, u32[]{:S(2)}, u32[]{:S(2)}) %collective-permute-start) | collective-permute-done | bytes 524320 | tf_op jit(solution)/shard_map/ppermute | solution.py:18
  27.8 8.6 %collective-permute-start.2 = (bf16[512,512]{1,0:T(8,128)(2,1)}, bf16[512,512]{1,0:T(8,128)(2,1)S(1)}, u32[]{:S(2)}, u32[]{:S(2)}) collective-permute-start(bf16[512,512]{1,0:T(8,128)(2,1)} %collective-permute-done), channel_id=1, source_target_pairs={{0,8},{8,16},{16,24},{24,0},{1,9},{9,17},{17,25},{25,1},{2,10},{10... | collective-permute-start | bytes 1572872 | tf_op jit(solution)/shard_map/ppermute | solution.py:18
  36.4 8.6 %all_gather.21 = bf16[128,2048]{1,0:T(8,128)(2,1)S(1)} all-gather(bf16[128,256]{1,0:T(8,128)(2,1)S(1)} %copy-done.12), channel_id=1, replica_groups=mesh['row'=4,'col'=8] {'col'}, dimensions={1}, use_global_device_ids=true | all-gather | bytes 589824 | tf_op jit(solution)/shard_map/all_gather | solution.py:72
  46.3 20.7 %collective-permute-done.1 = bf16[512,512]{1,0:T(8,128)(2,1)} collective-permute-done((bf16[512,512]{1,0:T(8,128)(2,1)}, bf16[512,512]{1,0:T(8,128)(2,1)}, u32[]{:S(2)}, u32[]{:S(2)}) %collective-permute-start.1) | collective-permute-done | bytes 524320 | tf_op jit(solution)/shard_map/ppermute | solution.py:21
  68.2 3.6 %collective-permute-done.2 = bf16[512,512]{1,0:T(8,128)(2,1)S(1)} collective-permute-done((bf16[512,512]{1,0:T(8,128)(2,1)}, bf16[512,512]{1,0:T(8,128)(2,1)S(1)}, u32[]{:S(2)}, u32[]{:S(2)}) %collective-permute-start.2) | collective-permute-done | bytes 524320 | tf_op jit(solution)/shard_map/ppermute | solution.py:18
  71.8 10.0 %all-gather.4.cloned.1.call-done = bf16[2048,512]{1,0:T(8,128)(2,1)} async-done(((bf16[512,512]{1,0:T(8,128)(2,1)}), bf16[2048,512]{1,0:T(8,128)(2,1)}) %all-gather.4.cloned.1.call-update) | async-done | bytes 2097168 | tf_op jit(solution)/shard_map/all_gather | solution.py:61
  88.3 30.7 %reduce-scatter.4.cloned.1.call-done = bf16[128,256]{1,0:T(8,128)(2,1)} async-done(((bf16[128,2048]{1,0:T(8,128)(2,1)}), bf16[128,256]{1,0:T(8,128)(2,1)}) %reduce-scatter.4.cloned.1.call-update) | async-done | bytes 65552 | tf_op jit(solution)/shard_map/reduce_scatter | solution.py:80
  120.1 10.9 %all_gather.23 = bf16[128,2048]{1,0:T(8,128)(2,1)S(1)} all-gather(bf16[128,256]{1,0:T(8,128)(2,1)S(1)} %get-tuple-element.14), channel_id=1, replica_groups=mesh['row'=4,'col'=8] {'col'}, dimensions={1}, use_global_device_ids=true | all-gather | bytes 589824 | tf_op jit(solution)/shard_map/all_gather | solution.py:72
  131.0 2.1 convolution_add_fusion
  133.1 2.2 convolution_convert_fusion.1
  135.4 34.2 %reduce-scatter.6.cloned.1.call-done = bf16[128,256]{1,0:T(8,128)(2,1)} async-done(((bf16[128,2048]{1,0:T(8,128)(2,1)}), bf16[128,256]{1,0:T(8,128)(2,1)}) %reduce-scatter.6.cloned.1.call-update) | async-done | bytes 65552 | tf_op jit(solution)/shard_map/reduce_scatter | solution.py:80
  170.7 12.2 %all-reduce = (f32[128]{0:T(128)S(1)}, f32[128]{0:T(128)S(1)}, f32[128]{0:T(128)S(1)}, f32[128]{0:T(128)S(1)}, f32[128]{0:T(128)S(1)}, /*index=5*/f32[128]{0:T(128)S(1)}) all-reduce(f32[128]{0:T(128)S(1)} %get-tuple-element.5, f32[128]{0:T(128)S(1)} %get-tuple-element.6, ...), channel_id=1, replica_groups=mesh['row'=4,'col'=8] {'col'}, use_global_device_ids=true, to_apply=%region_7.8 | all-reduce | flops 768 | bytes 6144 | tf_op jit(solution)/shard_map/psum | solution.py:45
  184.5 10.8 %all_gather.24 = bf16[128,2048]{1,0:T(8,128)(2,1)S(1)} all-gather(bf16[128,256]{1,0:T(8,128)(2,1)S(1)} %fusion.8), channel_id=1, replica_groups=mesh['row'=4,'col'=8] {'col'}, dimensions={1}, use_global_device_ids=true | all-gather | bytes 589824 | tf_op jit(solution)/shard_map/all_gather | solution.py:93
  196.1 2.4 fusion
  202.9 4.9 %all-to-all-start = ((bf16[2,128,2048]{1,0,2:T(2,128)(2,1)}), bf16[2,128,2048]{1,0,2:T(2,128)(2,1)S(1)}, u32[]{:S(2)}, u32[]{:S(2)}) async-start(bf16[2,128,2048]{1,0,2:T(2,128)(2,1)} %copy.11), calls=%async_computation.1 | async-start | bytes 2097152 | tf_op jit(solution)/shard_map/all_to_all | solution.py:119
  209.8 25.5 %reduce-scatter.8.cloned.1.call-done = bf16[128,256]{1,0:T(8,128)(2,1)} async-done(((bf16[128,2048]{1,0:T(8,128)(2,1)}), bf16[128,256]{1,0:T(8,128)(2,1)}) %reduce-scatter.8.cloned.1.call-update) | async-done | bytes 65552 | tf_op jit(solution)/shard_map/reduce_scatter | solution.py:104
  236.3 10.9 %all_gather.25 = bf16[128,2048]{1,0:T(8,128)(2,1)S(1)} all-gather(bf16[128,256]{1,0:T(8,128)(2,1)S(1)} %fusion.16), channel_id=1, replica_groups=mesh['row'=4,'col'=8] {'col'}, dimensions={1}, use_global_device_ids=true | all-gather | bytes 589824 | tf_op jit(solution)/shard_map/all_gather | solution.py:93
  249.3 4.6 %all-to-all-start.1 = ((bf16[2,128,2048]{1,0,2:T(2,128)(2,1)}), bf16[2,128,2048]{1,0,2:T(2,128)(2,1)S(1)}, u32[]{:S(2)}, u32[]{:S(2)}) async-start(bf16[2,128,2048]{1,0,2:T(2,128)(2,1)} %copy.13), calls=%async_computation.4 | async-start | bytes 2097152 | tf_op jit(solution)/shard_map/all_to_all | solution.py:114
  253.9 2.5 fusion.2
  258.4 33.8 %all-to-all-done.1 = bf16[2,128,2048]{1,0,2:T(2,128)(2,1)S(1)} async-done(((bf16[2,128,2048]{1,0,2:T(2,128)(2,1)}), bf16[2,128,2048]{1,0,2:T(2,128)(2,1)S(1)}, u32[]{:S(2)}, u32[]{:S(2)}) %all-to-all-start.1) | async-done | bytes 1048608 | tf_op jit(solution)/shard_map/all_to_all | solution.py:114
  293.1 2.9 convolution_bitcast_fusion
  296.0 8.5 %all-gather.6.cloned.1.call-done = bf16[2,512,512]{2,1,0:T(8,128)(2,1)} async-done(((bf16[2,128,512]{2,1,0:T(8,128)(2,1)}), bf16[2,512,512]{2,1,0:T(8,128)(2,1)}) %all-gather.6.cloned.1.call-update) | async-done | bytes 1048592 | tf_op jit(solution)/shard_map/all_gather | solution.py:122
  304.5 2.9 convolution_bitcast_fusion.1
  (70 shorter events, 29.6 us)
Async XLA Ops:
  7.2 37.8 %copy-start = (bf16[18,512]{1,0:T(8,128)(2,1)S(1)}, bf16[18,512]{1,0:T(8,128)(2,1)}, u32[]{:S(2)}) copy-start(bf16[18,512]{1,0:T(8,128)(2,1)} %param.11) | copy-start | bytes 55300
  7.2 7.0 %copy-start.9 = (bf16[512,512]{1,0:T(8,128)(2,1)S(1)}, bf16[512,512]{1,0:T(8,128)(2,1)}, u32[]{:S(2)}) copy-start(bf16[512,512]{1,0:T(8,128)(2,1)} %param.10) | copy-start | bytes 1572868
  7.2 29.2 %copy-start.12 = (bf16[128,256]{1,0:T(8,128)(2,1)S(1)}, bf16[128,256]{1,0:T(8,128)(2,1)}, u32[]{:S(2)}) copy-start(bf16[128,256]{1,0:T(8,128)(2,1)} %param.6) | copy-start | bytes 196612
  7.2 74.7 %all-gather.4.cloned.1.call-start = ((), (), s32[]{:S(2)}) async-start(), calls=%async_computation.5 | async-start | bytes 2621440 | tf_op jit(solution)/shard_map/all_gather | solution.py:61
  7.9 111.0 %reduce-scatter.4.cloned.1.call-start = ((), (), s32[]{:S(2)}) async-start(), calls=%async_computation.6 | async-start | bytes 589824 | tf_op jit(solution)/shard_map/reduce_scatter | solution.py:80
  8.0 19.8 %collective-permute-start = (bf16[512,512]{1,0:T(8,128)(2,1)}, bf16[512,512]{1,0:T(8,128)(2,1)}, u32[]{:S(2)}, u32[]{:S(2)}) collective-permute-start(bf16[512,512]{1,0:T(8,128)(2,1)} %param.10), channel_id=1, source_target_pairs={{0,8},{8,16},{16,24},{24,0},{1,9},{9,17},{17,25},{25,1},{2,10},{10... | collective-permute-start | bytes 1572872 | tf_op jit(solution)/shard_map/ppermute | solution.py:18
  11.1 56.0 %collective-permute-start.1 = (bf16[512,512]{1,0:T(8,128)(2,1)}, bf16[512,512]{1,0:T(8,128)(2,1)}, u32[]{:S(2)}, u32[]{:S(2)}) collective-permute-start(bf16[512,512]{1,0:T(8,128)(2,1)} %param.10), channel_id=1, source_target_pairs={{0,24},{8,0},{16,8},{24,16},{1,25},{9,1},{17,9},{25,17},{2,26},{10... | collective-permute-start | bytes 1572872 | tf_op jit(solution)/shard_map/ppermute | solution.py:21
  27.8 44.0 %collective-permute-start.2 = (bf16[512,512]{1,0:T(8,128)(2,1)}, bf16[512,512]{1,0:T(8,128)(2,1)S(1)}, u32[]{:S(2)}, u32[]{:S(2)}) collective-permute-start(bf16[512,512]{1,0:T(8,128)(2,1)} %collective-permute-done), channel_id=1, source_target_pairs={{0,8},{8,16},{16,24},{24,0},{1,9},{9,17},{17,25},{25,1},{2,10},{10... | collective-permute-start | bytes 1572872 | tf_op jit(solution)/shard_map/ppermute | solution.py:18
  71.8 12.1 %copy-start.2 = (bf16[512,2048]{1,0:T(8,128)(2,1)}, bf16[512,2048]{1,0:T(8,128)(2,1)S(1)}, u32[]{:S(2)}) copy-start(bf16[512,2048]{1,0:T(8,128)(2,1)S(1)} %constant_dynamic-update-slice_fusion) | copy-start | bytes 6291460
  85.2 45.8 %copy-start.1 = (bf16[2048,512]{1,0:T(8,128)(2,1)S(1)}, bf16[2048,512]{1,0:T(8,128)(2,1)}, u32[]{:S(2)}) copy-start(bf16[2048,512]{1,0:T(8,128)(2,1)} %all-gather.4.cloned.1.call-done) | copy-start | bytes 6291460
  85.2 84.4 %reduce-scatter.6.cloned.1.call-start = ((), (), s32[]{:S(2)}) async-start(), calls=%async_computation.7 | async-start | bytes 589824 | tf_op jit(solution)/shard_map/reduce_scatter | solution.py:80
  88.3 31.8 %copy-start.6 = (bf16[1,128,2048]{2,1,0:T(8,128)(2,1)}, bf16[1,128,2048]{2,1,0:T(8,128)(2,1)S(1)}, u32[]{:S(2)}) copy-start(bf16[1,128,2048]{2,1,0:T(8,128)(2,1)S(1)} %get-tuple-element.16) | copy-start | bytes 1572868
  119.0 14.2 %copy-start.3 = (bf16[512,2048]{1,0:T(8,128)(2,1)S(1)}, bf16[512,2048]{1,0:T(8,128)(2,1)}, u32[]{:S(2)}) copy-start(bf16[512,2048]{1,0:T(8,128)(2,1)} %copy-done.2) | copy-start | bytes 6291460
  135.3 99.9 %reduce-scatter.8.cloned.1.call-start = ((), (), s32[]{:S(2)}) async-start(), calls=%async_computation.8 | async-start | bytes 589824 | tf_op jit(solution)/shard_map/reduce_scatter | solution.py:104
  183.8 0.6 copy-start.7
  195.3 0.8 copy-start.4
  198.5 0.6 copy-start.10
  202.9 32.4 %copy-start.8 = (bf16[128,256]{1,0:T(8,128)(2,1)S(1)}, bf16[128,256]{1,0:T(8,128)(2,1)}, u32[]{:S(2)}) copy-start(bf16[128,256]{1,0:T(8,128)(2,1)} %copy-done.7) | copy-start | bytes 196612
  202.9 44.2 %copy-start.5 = (bf16[128,2048]{1,0:T(8,128)(2,1)S(1)}, bf16[128,2048]{1,0:T(8,128)(2,1)}, u32[]{:S(2)}) copy-start(bf16[128,2048]{1,0:T(8,128)(2,1)} %copy-done.4) | copy-start | bytes 1572868
  202.9 46.3 %all-to-all-start = ((bf16[2,128,2048]{1,0,2:T(2,128)(2,1)}), bf16[2,128,2048]{1,0,2:T(2,128)(2,1)S(1)}, u32[]{:S(2)}, u32[]{:S(2)}) async-start(bf16[2,128,2048]{1,0,2:T(2,128)(2,1)} %copy.11), calls=%async_computation.1 | async-start | bytes 2097152 | tf_op jit(solution)/shard_map/all_to_all | solution.py:119
  207.9 85.2 %all-gather.8.cloned.1.call-start = ((), (), s32[]{:S(2)}) async-start(), calls=%async_computation.10 | async-start | bytes 1310720 | tf_op jit(solution)/shard_map/all_gather | solution.py:115
  249.3 43.0 %all-to-all-start.1 = ((bf16[2,128,2048]{1,0,2:T(2,128)(2,1)}), bf16[2,128,2048]{1,0,2:T(2,128)(2,1)S(1)}, u32[]{:S(2)}, u32[]{:S(2)}) async-start(bf16[2,128,2048]{1,0,2:T(2,128)(2,1)} %copy.13), calls=%async_computation.4 | async-start | bytes 2097152 | tf_op jit(solution)/shard_map/all_to_all | solution.py:114
  253.9 2.5 copy-start.11
  253.9 50.6 %all-gather.6.cloned.1.call-start = ((), (), s32[]{:S(2)}) async-start(), calls=%async_computation.9 | async-start | bytes 1310720 | tf_op jit(solution)/shard_map/all_gather | solution.py:122
Sparse Core Ops, SparseCore 0:
  9.6 72.2 all-gather.3
  85.5 33.4 reduce-scatter.3
  135.5 34.1 reduce-scatter.5
  200.9 34.2 reduce-scatter.7
  236.7 37.5 all-gather.7
  275.7 28.8 all-gather.5
